TPU v7x, 256 devices: a whole 4x4x8 slice. The times are simulated.
256 devices in a mesh: section: 16 (over z, core), mp: 8 (over x, y_hi), dp: 2 (over y_lo).
Axes of the slice: x: 4, y: 4 (y_hi: 2, y_lo: 2; y = y_hi * 2 + y_lo), z: 8, core: 2. Of those that a mesh axis runs over, the one named last changes fastest.
Arguments:
- enc_out: bfloat16 [2, 512, 4096], P('dp', 'mp', 'section'), may hold values from -6 to 6
- kv_weight: bfloat16 [16, 4096, 2, 4096], P('section', None, None, 'mp'), may hold values from -0.09375 to 0.09375
- dec_query: bfloat16 [16, 2, 512, 4096], P('section', 'dp', None, 'mp'), may hold values from -120 to 120
- ctx_grad: bfloat16 [16, 2, 512, 4096], P('section', 'dp', None, 'mp'), may hold values from -6 to 6
- enc_seg: int32 [2, 512], P('dp'), may hold values from 0 to 7, never falling along the last dimension, each value on 1 to 128 neighbouring positions
- dec_seg: int32 [2, 512], P('dp'), may hold values from 0 to 7, never falling along the last dimension, each value on 1 to 128 neighbouring positions
Outputs:
- context: bfloat16 [16, 2, 512, 4096], P('section', 'dp', None, 'mp')
- enc_grad: float32 [2, 512, 4096], P('dp', 'mp', 'section')
Inputs may be any that keep to these rules, and one draw needn't show every extreme that they name: `enc_seg`: document ids never fall along a sequence and every id appears. `dec_seg`: document ids never fall along a sequence and every id appears.
All inputs are finite; a program needn't handle non-finite values.
Results may differ from a plain program's by a relative error of at most 0.04.
The roundings to bfloat16 on the way count: a program that leaves them out, or rounds other values in their place, can miss the bound.
Values may be sent and summed in bfloat16 or wider, within the bound.
No kernel may reach another device: no remote copies, remote signals or barrier semaphores. Data moves between devices by JAX's collectives and lax.ppermute only.
A program may use at most 128 MiB of HBM per device.

v0:
```python
import jax
import jax.numpy as jnp
from jax import lax
from jax.sharding import PartitionSpec as P

HD = 256


def attend(query, keys, values, grad, same_doc):
    scale = HD ** (-0.5)
    scores = jnp.einsum("qhd,khd->hqk", query, keys, preferred_element_type=jnp.float32) * scale
    scores = jnp.where(same_doc[None], scores, -1e30)
    top_score = jnp.max(scores, axis=-1, keepdims=True)
    raised = jnp.exp(scores - top_score)
    probs = raised / jnp.sum(raised, axis=-1, keepdims=True)
    probs_low = probs.astype(jnp.bfloat16)
    context = jnp.einsum(
        "hqk,khd->qhd", probs_low, values, preferred_element_type=jnp.float32
    ).astype(jnp.bfloat16)
    grad_values = jnp.einsum(
        "hqk,qhd->khd", probs_low, grad, preferred_element_type=jnp.float32
    ).astype(jnp.bfloat16)
    grad_probs = jnp.einsum("qhd,khd->hqk", grad, values, preferred_element_type=jnp.float32)
    inner_sum = jnp.sum(probs * grad_probs, axis=-1, keepdims=True)
    grad_scores = (probs * (grad_probs - inner_sum) * scale).astype(jnp.bfloat16)
    grad_keys = jnp.einsum(
        "hqk,qhd->khd", grad_scores, query, preferred_element_type=jnp.float32
    ).astype(jnp.bfloat16)
    return (context, grad_keys, grad_values)


def per_device(enc_out, kv_weight, dec_query, ctx_grad, enc_seg, dec_seg):
    shard_rows = enc_out[0]
    width = kv_weight.shape[3]
    model_width = kv_weight.shape[1]
    flat_weight = kv_weight[0].reshape(model_width, 2 * width)
    all_tokens = lax.all_gather(shard_rows, "mp", axis=0, tiled=True)
    weight_rows = flat_weight
    key_values = jnp.dot(
        lax.all_gather(all_tokens, "section", axis=1, tiled=True),
        weight_rows,
        preferred_element_type=jnp.float32,
    ).astype(jnp.bfloat16)
    length = key_values.shape[0]
    heads_here = width // HD
    decoder = dec_query.shape[2]
    keys = key_values[:, :width].reshape(length, heads_here, HD)
    values = key_values[:, width:].reshape(length, heads_here, HD)
    same_doc = dec_seg[0][:, None] == enc_seg[0][None, :]
    query = dec_query[0, 0].reshape(decoder, heads_here, HD)
    grad = ctx_grad[0, 0].reshape(decoder, heads_here, HD)
    context, grad_keys, grad_values = attend(query, keys, values, grad, same_doc)
    grad_both = jnp.concatenate(
        [grad_keys.reshape(length, width), grad_values.reshape(length, width)], axis=1
    )
    weight_rows = flat_weight
    feature_share = lax.psum_scatter(
        lax.dot_general(
            weight_rows, grad_both, (((1,), (1,)), ((), ())), preferred_element_type=jnp.float32
        ).astype(jnp.bfloat16),
        "section",
        scatter_dimension=0,
        tiled=True,
    )
    owned_grad = (
        lax.psum_scatter(feature_share, "mp", scatter_dimension=1, tiled=True).astype(jnp.float32).T
    )
    return (context.reshape(1, 1, decoder, width), owned_grad[None])


def solution(mesh):
    placed = (
        P("dp", "mp", "section"),
        P("section", None, None, "mp"),
        P("section", "dp", None, "mp"),
        P("section", "dp", None, "mp"),
        P("dp", None),
        P("dp", None),
    )
    return jax.shard_map(
        per_device,
        mesh=mesh,
        in_specs=placed,
        out_specs=(P("section", "dp", None, "mp"), P("dp", "mp", "section")),
        check_vma=False,
    )
```

profile of v0, /device:TPU:2, one launch (start us, length us, event | category | flops | bytes accessed | tf_op | source)
XLA Modules:
  0.0 273.9 jit_solution(1828879622895667745)
XLA Ops:
  7.2 0.0 all-gather.4.cloned.1.call-start
  7.2 36.3 %all-gather = bf16[1,512,256]{2,1,0:T(8,128)(2,1)} all-gather(bf16[1,64,256]{2,1,0:T(8,128)(2,1)} %param.6), channel_id=2, replica_groups=mesh['section'=16,'mp'=8,'dp'=2] {'mp'}, dimensions={1}, use_global_device_ids=true | all-gather | bytes 294912 | tf_op jit(solution)/shard_map/all_gather | solution.py:37
  43.5 0.0 all-gather.4.cloned.1.call-update
  43.5 0.0 reduce-scatter.3.cloned.1.call-start
  43.6 2.1 copy.23
  45.7 1.3 copy.24
  46.9 9.5 %copy.27 = bf16[512,8,2,512]{3,1,2,0:T(8,128)(2,1)} copy(bf16[512,8,2,512]{3,2,1,0:T(2,128)(2,1)} %bitcast.75) | data formatting | bytes 16777216
  56.4 0.2 broadcast_compare_fusion
  56.6 38.7 %all-gather.4.cloned.1.call-done = bf16[1,512,4096]{2,1,0:T(8,128)(2,1)} async-done(((bf16[1,512,256]{2,1,0:T(8,128)(2,1)}), bf16[1,512,4096]{2,1,0:T(8,128)(2,1)}) %all-gather.4.cloned.1.call-update) | async-done | bytes 4194320 | tf_op jit(solution)/shard_map/all_gather | solution.py:40
  95.3 9.1 %fusion.10 = bf16[512,1024]{1,0:T(8,128)(2,1)S(1)} fusion(bf16[4096,1024]{1,0:T(8,128)(2,1)} %bitcast.76, bf16[1,512,4096]{2,1,0:T(8,128)(2,1)} %all-gather.4.cloned.1.call-done), kind=kOutput, calls=%fused_computation.15 | convolution fusion | flops 4295491584 | bytes 13631488 | tf_op jit(solution)/shard_map/dot_general | solution.py:39
  104.5 0.9 fusion.43
  105.3 0.4 fusion.26
  105.8 3.5 %fusion.44 = (f32[2,512]{1,0:T(2,128)S(1)}, f32[2,512,512]{1,2,0:T(8,128)}) fusion(pred[512,512]{0,1:T(8,128)(4,1)S(1)} %broadcast_compare_fusion, bf16[512,2,256]{0,2,1:T(8,128)(2,1)} %bitcast.82, bf16[64,2,8,256]{3,2,1,0:T(8,128)(2,1)} %bitcast.85), kind=kOutput, calls=%fused_computation.46 | convolution fusion | flops 270533120 | bytes 3411968 | tf_op jit(solution)/shard_map/sub | solution.py:14
  109.2 2.9 %convolution_convert_fusion.1 = bf16[2,512,256]{1,2,0:T(8,128)(2,1)} fusion(bf16[512,2,256]{0,2,1:T(8,128)(2,1)S(1)} %bitcast.79, f32[2,512,512]{1,2,0:T(8,128)} %get-tuple-element.7, f32[2,512]{1,0:T(2,128)S(1)} %get-tuple-element.6), kind=kOutput, calls=%fused_computation.17 | convolution fusion | flops 269746176 | bytes 3149824 | tf_op jit(solution)/shard_map/hqk,qhd->khd/dot_general | solution.py:20
  112.1 4.2 %fusion.13 = bf16[2,512,256]{1,2,0:T(8,128)(2,1)} fusion(bf16[512,2,256]{0,2,1:T(8,128)(2,1)} %bitcast.83, f32[2,512,512]{2,1,0:T(8,128)S(1)} %fusion.26, f32[2,512,512]{1,2,0:T(8,128)} %get-tuple-element.7, f32[2,512]{1,0:T(2,128)S(1)} %get-tuple-element.6), kind=kOutput, calls=%fused_computation.16 | convolution fusion | flops 272369152 | bytes 5246976 | tf_op jit(solution)/shard_map/hqk,qhd->khd/dot_general | solution.py:26
  116.3 10.4 %fusion.2 = bf16[4096,512]{0,1:T(8,128)(2,1)} fusion(bf16[4096,1024]{1,0:T(8,128)(2,1)} %bitcast.77, bf16[512,512]{0,1:T(8,128)(2,1)S(1)} %bitcast.88, bf16[512,512]{0,1:T(8,128)(2,1)} %bitcast.89), kind=kOutput, calls=%fused_computation.3 | convolution fusion | flops 4299161600 | bytes 13631488 | tf_op jit(solution)/shard_map/dot_general | solution.py:58
  126.7 0.0 reduce-scatter.3.cloned.1.call-update
  126.7 0.0 reduce-scatter.5.cloned.1.call-start
  126.8 62.2 %reduce-scatter.3.cloned.1.call-done = bf16[256,512]{0,1:T(8,128)(2,1)} async-done(((bf16[4096,512]{0,1:T(8,128)(2,1)}), bf16[256,512]{0,1:T(8,128)(2,1)}) %reduce-scatter.3.cloned.1.call-update) | async-done | bytes 262160 | tf_op jit(solution)/shard_map/reduce_scatter | solution.py:57
  189.0 0.0 reduce-scatter.5.cloned.1.call-update
  189.0 0.5 convolution_convert_fusion.2
  189.5 1.0 copy.19
  190.5 75.5 %reduce-scatter.5.cloned.1.call-done = bf16[256,64]{0,1:T(8,128)(2,1)} async-done(((bf16[256,512]{0,1:T(8,128)(2,1)}), bf16[256,64]{0,1:T(8,128)(2,1)}) %reduce-scatter.5.cloned.1.call-update) | async-done | bytes 32784 | tf_op jit(solution)/shard_map/reduce_scatter | solution.py:66
  266.0 1.4 convert_bitcast_fusion
  (8 shorter events, 0.0 us)
Async XLA Ops:
  7.2 88.1 %all-gather.4.cloned.1.call-start = ((), (), s32[]{:S(2)}) async-start(), calls=%async_computation.4 | async-start | bytes 4456448 | tf_op jit(solution)/shard_map/all_gather | solution.py:40
  43.5 145.5 %reduce-scatter.3.cloned.1.call-start = ((), (), s32[]{:S(2)}) async-start(), calls=%async_computation.2 | async-start | bytes 4456448 | tf_op jit(solution)/shard_map/reduce_scatter | solution.py:57
  46.9 9.5 %copy-start = (s32[1,512]{1,0:T(1,128)S(1)}, s32[1,512]{1,0:T(1,128)}, u32[]{:S(2)}) copy-start(s32[1,512]{1,0:T(1,128)} %param.11) | copy-start | bytes 6148
  46.9 9.5 %copy-start.1 = (s32[1,512]{1,0:T(1,128)S(1)}, s32[1,512]{1,0:T(1,128)}, u32[]{:S(2)}) copy-start(s32[1,512]{1,0:T(1,128)} %param.10) | copy-start | bytes 6148
  112.1 4.2 %copy-start.2 = (bf16[2,512,256]{1,2,0:T(8,128)(2,1)S(1)}, bf16[2,512,256]{1,2,0:T(8,128)(2,1)}, u32[]{:S(2)}) copy-start(bf16[2,512,256]{1,2,0:T(8,128)(2,1)} %convolution_convert_fusion.1) | copy-start | bytes 1572868
  126.7 62.3 %copy-start.3 = (f32[2,512,512]{1,2,0:T(8,128)S(1)}, f32[2,512,512]{1,2,0:T(8,128)}, u32[]{:S(2)}) copy-start(f32[2,512,512]{1,2,0:T(8,128)} %get-tuple-element.7) | copy-start | bytes 6291460
  126.7 139.3 %reduce-scatter.5.cloned.1.call-start = ((), (), s32[]{:S(2)}) async-start(), calls=%async_computation.3 | async-start | bytes 294912 | tf_op jit(solution)/shard_map/reduce_scatter | solution.py:66
Sparse Core Ops, SparseCore 0:
  43.6 51.6 all-gather.3
  126.8 62.1 reduce-scatter.2
  192.9 73.1 reduce-scatter.4
where the time goes:
time: 274 us
  waiting for transfers between devices  176 us (64%)
  blocking collectives  36.3 us (13%)
  matrix products  31 us (11%)
  local copies, waits for them, and re-layouts  14.7 us (5%)
  between operations  13.8 us (5%)
    reduce_scatter x1, waiting for transfers between devices, per_device(): lax.psum_scatter(feature_share, 'mp', scatter_dimension=1, tiled=True)  75.5 us
    reduce_scatter x1, waiting for transfers between devices, per_device(): lax.psum_scatter(lax.dot_general(weight_rows, grad_both, (((1,), (1,)), (...  62.2 us
    all_gather x1, waiting for transfers between devices, per_device(): lax.all_gather(all_tokens, 'section', axis=1, tiled=True)  38.7 us
    all_gather x1, blocking collectives, per_device(): all_tokens = lax.all_gather(shard_rows, 'mp', axis=0, tiled=True)  36.3 us
    unnamed x10, local copies, waits for them, and re-layouts  10.5 us
    dot_general x1, matrix products, per_device(): lax.dot_general(weight_rows, grad_both, (((1,), (1,)), ((), ())), preferr...  10.4 us
    dot_general x1, matrix products, per_device(): jnp.dot(lax.all_gather(all_tokens, 'section', axis=1, tiled=True), weight...  9.14 us
  transfers between devices with their start and end apart: 3, of which 3 were waited for; matrix products, arithmetic and copies ran while one was open for 5% of the time, Pallas kernels for 0%

commit v1 on v0

--- a/solution.py
+++ b/solution.py
@@ -34,7 +34,10 @@
     width = kv_weight.shape[3]
     model_width = kv_weight.shape[1]
     flat_weight = kv_weight[0].reshape(model_width, 2 * width)
-    all_tokens = lax.all_gather(shard_rows, "mp", axis=0, tiled=True)
+    size = lax.axis_size("mp")
+    blocks = jnp.stack([shard_rows for _ in range(size)])
+    blocks = lax.all_to_all(blocks, "mp", split_axis=0, concat_axis=0)
+    all_tokens = jnp.concatenate(blocks, axis=0)
     weight_rows = flat_weight
     key_values = jnp.dot(
         lax.all_gather(all_tokens, "section", axis=1, tiled=True),

time: 274 us -> 250 us (0.912)
  blocking collectives: 36.3 us -> 14.4 us
    all_gather x1 -> x0, blocking collectives: 36.3 us -> none  [per_device(): all_tokens = lax.all_gather(shard_rows, 'mp', axis=0, tiled=True)]
    all_to_all x0 -> x1, blocking collectives: none -> 14.4 us  [per_device(): blocks = lax.all_to_all(blocks, 'mp', split_axis=0, concat_axis=0)]
    unnamed x10 -> x12, local copies, waits for them, and re-layouts: 10.5 us -> 10.5 us
where the time goes in v1:
time: 250 us
  waiting for transfers between devices  175 us (70%)
  matrix products  30.9 us (12%)
  local copies, waits for them, and re-layouts  14.5 us (6%)
  blocking collectives  14.4 us (6%)
  between operations  13.8 us (6%)
    reduce_scatter x1, waiting for transfers between devices, per_device(): lax.psum_scatter(feature_share, 'mp', scatter_dimension=1, tiled=True)  75.6 us
    reduce_scatter x1, waiting for transfers between devices, per_device(): lax.psum_scatter(lax.dot_general(weight_rows, grad_both, (((1,), (1,)), (...  62.2 us
    all_gather x1, waiting for transfers between devices, per_device(): lax.all_gather(all_tokens, 'section', axis=1, tiled=True)  36.7 us
    all_to_all x1, blocking collectives, per_device(): blocks = lax.all_to_all(blocks, 'mp', split_axis=0, concat_axis=0)  14.4 us
    unnamed x12, local copies, waits for them, and re-layouts  10.5 us
    dot_general x1, matrix products, per_device(): lax.dot_general(weight_rows, grad_both, (((1,), (1,)), ((), ())), preferr...  10.4 us
    dot_general x1, matrix products, per_device(): jnp.dot(lax.all_gather(all_tokens, 'section', axis=1, tiled=True), weight...  9.14 us
  transfers between devices with their start and end apart: 3, of which 3 were waited for; matrix products, arithmetic and copies ran while one was open for 5% of the time, Pallas kernels for 0%

profile of v1, /device:TPU:2, one launch (start us, length us, event | category | flops | bytes accessed | tf_op | source)
XLA Modules:
  0.0 250.0 jit_solution(13774118292123539973)
XLA Ops:
  7.2 0.0 all-gather.2.cloned.1.call-start
  7.2 0.8 stack.3
  8.0 14.4 %all_to_all.5 = bf16[8,64,256]{2,1,0:T(8,128)(2,1)} all-to-all(bf16[8,64,256]{2,1,0:T(8,128)(2,1)S(1)} %stack.3), channel_id=1, replica_groups=mesh['section'=16,'mp'=8,'dp'=2] {'mp'}, dimensions={0} | all-to-all | bytes 524288 | tf_op jit(solution)/shard_map/all_to_all | solution.py:39
  22.4 0.0 all-gather.2.cloned.1.call-update
  22.5 0.0 reduce-scatter.3.cloned.1.call-start
  22.5 2.1 copy.23
  24.6 0.2 copy.24
  24.8 9.5 %copy.27 = bf16[512,8,2,512]{3,1,2,0:T(8,128)(2,1)} copy(bf16[512,8,2,512]{3,2,1,0:T(2,128)(2,1)} %bitcast.73) | data formatting | bytes 16777216
  34.3 0.2 broadcast_compare_fusion
  34.5 36.7 %all-gather.2.cloned.1.call-done = bf16[512,4096]{1,0:T(8,128)(2,1)} async-done(((bf16[512,256]{1,0:T(8,128)(2,1)}), bf16[512,4096]{1,0:T(8,128)(2,1)}) %all-gather.2.cloned.1.call-update) | async-done | bytes 4194320 | tf_op jit(solution)/shard_map/all_gather | solution.py:43
  71.2 9.1 %convolution_convert_fusion.1 = bf16[512,1024]{1,0:T(8,128)(2,1)S(1)} fusion(bf16[512,4096]{1,0:T(8,128)(2,1)} %all-gather.2.cloned.1.call-done, bf16[4096,1024]{1,0:T(8,128)(2,1)} %bitcast.74), kind=kOutput, calls=%fused_computation.13 | convolution fusion | flops 4295491584 | bytes 13631488 | tf_op jit(solution)/shard_map/dot_general | solution.py:42
  80.4 0.9 fusion.38
  81.2 0.4 fusion.21
  81.7 3.5 %fusion.39 = (f32[2,512]{1,0:T(2,128)S(1)}, f32[2,512,512]{1,2,0:T(8,128)}) fusion(pred[512,512]{0,1:T(8,128)(4,1)S(1)} %broadcast_compare_fusion, bf16[512,2,256]{0,2,1:T(8,128)(2,1)} %bitcast.81, bf16[64,2,8,256]{3,2,1,0:T(8,128)(2,1)} %bitcast.84), kind=kOutput, calls=%fused_computation.44 | convolution fusion | flops 270533120 | bytes 3411968 | tf_op jit(solution)/shard_map/sub | solution.py:14
  85.1 2.9 %convolution_convert_fusion.2 = bf16[2,512,256]{1,2,0:T(8,128)(2,1)} fusion(bf16[512,2,256]{0,2,1:T(8,128)(2,1)S(1)} %bitcast.77, f32[2,512,512]{1,2,0:T(8,128)} %get-tuple-element.7, f32[2,512]{1,0:T(2,128)S(1)} %get-tuple-element.6), kind=kOutput, calls=%fused_computation.15 | convolution fusion | flops 269746176 | bytes 3149824 | tf_op jit(solution)/shard_map/hqk,qhd->khd/dot_general | solution.py:20
  88.0 4.2 %fusion.8 = bf16[2,512,256]{1,2,0:T(8,128)(2,1)} fusion(bf16[512,2,256]{0,2,1:T(8,128)(2,1)} %bitcast.82, f32[2,512,512]{2,1,0:T(8,128)S(1)} %fusion.21, f32[2,512,512]{1,2,0:T(8,128)} %get-tuple-element.7, f32[2,512]{1,0:T(2,128)S(1)} %get-tuple-element.6), kind=kOutput, calls=%fused_computation.14 | convolution fusion | flops 272369152 | bytes 5246976 | tf_op jit(solution)/shard_map/hqk,qhd->khd/dot_general | solution.py:26
  92.2 10.4 %fusion.2 = bf16[4096,512]{0,1:T(8,128)(2,1)} fusion(bf16[4096,1024]{1,0:T(8,128)(2,1)} %bitcast.75, bf16[512,512]{0,1:T(8,128)(2,1)S(1)} %bitcast.88, bf16[512,512]{0,1:T(8,128)(2,1)} %bitcast.89), kind=kOutput, calls=%fused_computation.3 | convolution fusion | flops 4299161600 | bytes 13631488 | tf_op jit(solution)/shard_map/dot_general | solution.py:61
  102.6 0.0 reduce-scatter.3.cloned.1.call-update
  102.6 0.0 reduce-scatter.5.cloned.1.call-start
  102.7 62.2 %reduce-scatter.3.cloned.1.call-done = bf16[256,512]{0,1:T(8,128)(2,1)} async-done(((bf16[4096,512]{0,1:T(8,128)(2,1)}), bf16[256,512]{0,1:T(8,128)(2,1)}) %reduce-scatter.3.cloned.1.call-update) | async-done | bytes 262160 | tf_op jit(solution)/shard_map/reduce_scatter | solution.py:60
  164.9 0.5 convolution_convert_fusion.3
  165.4 1.0 copy.19
  166.4 75.6 %reduce-scatter.5.cloned.1.call-done = bf16[256,64]{0,1:T(8,128)(2,1)} async-done(((bf16[256,512]{0,1:T(8,128)(2,1)}), bf16[256,64]{0,1:T(8,128)(2,1)}) %reduce-scatter.5.cloned.1.call-update) | async-done | bytes 32784 | tf_op jit(solution)/shard_map/reduce_scatter | solution.py:69
  242.0 1.4 convert_bitcast_fusion
  (11 shorter events, 0.0 us)
Async XLA Ops:
  7.2 17.4 %copy-start = (bf16[1,1,512,512]{3,2,1,0:T(8,128)(2,1)S(1)}, bf16[1,1,512,512]{3,2,1,0:T(8,128)(2,1)}, u32[]{:S(2)}) copy-start(bf16[1,1,512,512]{3,2,1,0:T(8,128)(2,1)} %param.9) | copy-start | bytes 1572868
  7.2 64.0 %all-gather.2.cloned.1.call-start = ((), (), s32[]{:S(2)}) async-start(), calls=%async_computation.3 | async-start | bytes 4456448 | tf_op jit(solution)/shard_map/all_gather | solution.py:43
  22.5 142.4 %reduce-scatter.3.cloned.1.call-start = ((), (), s32[]{:S(2)}) async-start(), calls=%async_computation.4 | async-start | bytes 4456448 | tf_op jit(solution)/shard_map/reduce_scatter | solution.py:60
  24.8 9.5 %copy-start.1 = (s32[1,512]{1,0:T(1,128)S(1)}, s32[1,512]{1,0:T(1,128)}, u32[]{:S(2)}) copy-start(s32[1,512]{1,0:T(1,128)} %param.11) | copy-start | bytes 6148
  24.8 9.5 %copy-start.2 = (s32[1,512]{1,0:T(1,128)S(1)}, s32[1,512]{1,0:T(1,128)}, u32[]{:S(2)}) copy-start(s32[1,512]{1,0:T(1,128)} %param.10) | copy-start | bytes 6148
  88.0 4.2 %copy-start.3 = (bf16[2,512,256]{1,2,0:T(8,128)(2,1)S(1)}, bf16[2,512,256]{1,2,0:T(8,128)(2,1)}, u32[]{:S(2)}) copy-start(bf16[2,512,256]{1,2,0:T(8,128)(2,1)} %convolution_convert_fusion.2) | copy-start | bytes 1572868
  102.6 62.3 %copy-start.4 = (f32[2,512,512]{1,2,0:T(8,128)S(1)}, f32[2,512,512]{1,2,0:T(8,128)}, u32[]{:S(2)}) copy-start(f32[2,512,512]{1,2,0:T(8,128)} %get-tuple-element.7) | copy-start | bytes 6291460
  102.6 139.4 %reduce-scatter.5.cloned.1.call-start = ((), (), s32[]{:S(2)}) async-start(), calls=%async_computation.5 | async-start | bytes 294912 | tf_op jit(solution)/shard_map/reduce_scatter | solution.py:69
Sparse Core Ops, SparseCore 0:
  22.6 48.5 all-gather.1
  102.7 62.1 reduce-scatter.2
  168.7 73.2 reduce-scatter.4
